TPU v7x, 256 devices: a whole 4x4x8 slice. The times are simulated.
256 devices in a mesh: mem: 16 (over z_hi, x, core), lev: 16 (over y, z_lo).
Axes of the slice: x: 4, y: 4, z: 8 (z_hi: 2, z_lo: 4; z = z_hi * 4 + z_lo), core: 2. Of those that a mesh axis runs over, the one named last changes fastest.
Arguments:
- alpha_weights: float32 [16, 32, 384, 512], P('mem', 'lev'), may hold values from -6 to 6
- perturbations: bfloat16 [16, 32, 393216], P('mem', None, 'lev'), may hold values from -6 to 6
- coef_x: float32 [384, 512], replicated, may hold values from 0.02 to 0.24
- coef_y: float32 [384, 512], replicated, may hold values from 0.02 to 0.24
- level_scale: float32 [32], replicated, may hold values from 0.3 to 1
- level_map: int32 [32], replicated, may hold values from 0 to 31, each once
- tile_widths: int32 [16], replicated, may hold values from 1 to 24576, 196608 in all
- band_widths: int32 [32], replicated, may hold values from 1 to 4, as said below
Outputs:
- increment: float32 [32, 393216], P('mem', 'lev')
Inputs may be any that keep to these rules, and one draw needn't show every extreme that they name: `level_map`: a permutation of the levels. `tile_widths`: sum to 196608; the largest equals 24576. `band_widths`: some level has a band of exactly 4.
All inputs are finite; a program needn't handle non-finite values.
Results may differ from a plain program's by a relative error of at most 0.0035.
Values may be sent and summed in bfloat16 or wider, within the bound.
No kernel may reach another device: no remote copies, remote signals or barrier semaphores. Data moves between devices by JAX's collectives and lax.ppermute only.
A program may use at most 64 MiB of HBM per device.

v0:
```python
import jax
import jax.numpy as jnp
from jax import lax
from jax.sharding import PartitionSpec as P

STEPS = 16


def diffuse_level(layer_field, scaled_x, scaled_y):

    def step_once(index_step, state):
        flux_x = scaled_x[:-1, :] * (state[1:, :] - state[:-1, :])
        flux_y = scaled_y[:, :-1] * (state[:, 1:] - state[:, :-1])
        zero_row = jnp.zeros((1, state.shape[1]), state.dtype)
        zero_col = jnp.zeros((state.shape[0], 1), state.dtype)
        change = jnp.concatenate([flux_x, zero_row], 0) - jnp.concatenate([zero_row, flux_x], 0)
        change = (
            change + jnp.concatenate([flux_y, zero_col], 1) - jnp.concatenate([zero_col, flux_y], 1)
        )
        return state + change

    return lax.fori_loop(0, STEPS, step_once, layer_field)


def vertical_matrix(band_widths):
    level_pos = jnp.arange(band_widths.shape[0])
    distance = jnp.abs(level_pos[:, None] - level_pos[None, :]).astype(jnp.float32)
    mutual = jnp.minimum(band_widths[:, None], band_widths[None, :]).astype(jnp.float32)
    return jnp.where(distance <= mutual, jnp.exp(-distance * distance / (mutual * mutual)), 0.0)


def body(
    alpha_weights, perturbations, coef_x, coef_y, level_scale, level_map, tile_widths, band_widths
):
    mem_dev, lev_dev, rows_x, rows_y = alpha_weights.shape
    levels = perturbations.shape[1]
    capacity = perturbations.shape[2]
    tile_count = lax.axis_size("lev")
    member_devices = lax.axis_size("mem")
    level_ids = jnp.arange(levels)
    slot_ids = lax.axis_index("lev") * lev_dev + jnp.arange(lev_dev)
    owned_levels = jnp.sum(
        jnp.where(slot_ids[:, None] == level_ids[None, :], level_map[None, :], 0), axis=1
    )
    level_gain = jnp.sum(
        jnp.where(owned_levels[:, None] == level_ids[None, :], level_scale[None, :], 0.0), axis=1
    )

    def smooth_slot(member_field, strength):
        return diffuse_level(member_field, coef_x * strength, coef_y * strength)

    smoothed = jax.vmap(jax.vmap(smooth_slot, (0, 0)), (0, None))(alpha_weights, level_gain)
    rounded = smoothed.astype(jnp.bfloat16).reshape(mem_dev, lev_dev, rows_x * rows_y)
    padded = jnp.pad(rounded, ((0, 0), (0, 0), (0, capacity)))
    starts = jnp.cumsum(tile_widths) - tile_widths

    def cut_tile(first_col):
        return lax.dynamic_slice_in_dim(padded, first_col, capacity, 2)

    outgoing = jax.vmap(cut_tile, out_axes=1)(starts)
    arrived = lax.all_to_all(outgoing, "lev", split_axis=1, concat_axis=1, tiled=True).reshape(
        mem_dev, levels, capacity
    )
    own_width = jnp.sum(jnp.where(jnp.arange(tile_count) == lax.axis_index("lev"), tile_widths, 0))
    valid_cols = jnp.arange(capacity) < own_width
    localizer = vertical_matrix(band_widths).astype(jnp.bfloat16)
    perm_onehot = (level_ids[:, None] == level_map[None, :]).astype(jnp.bfloat16)
    permuted = jnp.dot(localizer, perm_onehot, preferred_element_type=jnp.float32).astype(
        jnp.bfloat16
    )
    share_rows = levels // member_devices
    spread = jnp.einsum("ks,msc->mkc", permuted, arrived, preferred_element_type=jnp.float32)
    pert_rows = perturbations.astype(jnp.float32)
    summed = lax.psum(
        jnp.where(valid_cols[None, :], jnp.sum(pert_rows * spread, axis=0), 0.0), "mem"
    )
    result = lax.dynamic_slice_in_dim(summed, lax.axis_index("mem") * share_rows, share_rows, 0)
    return result


def solution(mesh):
    placed = (P("mem", "lev", None, None), P("mem", None, "lev"), P(), P(), P(), P(), P(), P())
    return jax.shard_map(
        body, mesh=mesh, in_specs=placed, out_specs=P("mem", "lev"), check_vma=False
    )
```

profile of v0, /device:TPU:8, one launch (start us, length us, event | category | flops | bytes accessed | tf_op | source)
XLA Modules:
  0.0 338.8 jit_solution(3615929898913939918)
XLA Ops:
  7.6 3.1 broadcast_multiply_fusion
  10.7 44.0 %while.11 = (s32[]{:T(128)}, f32[1,2,384,512]{3,2,1,0:T(8,128)S(1)}, f32[2,384,512]{2,1,0:T(8,128)}, f32[2,384,512]{2,1,0:T(8,128)S(1)}, s32[]{:T(128)}) while((s32[]{:T(128)}, f32[1,2,384,512]{3,2,1,0:T(8,128)S(1)}, f32[2,384,512]{2,1,0:T(8,128)}, f32[2,384,512]{2,1,0:T(8,128)S(1)}, s32[]{:T(128)}) %tuple.39), condition=%wide.region_4.5_spmd, body=%wide.region_3.4_spmd.sunk | while | flops 3142146 | bytes 25130072 | solution.py:22
  57.7 33.7 %while.12 = (s32[]{:T(128)}, bf16[1,2,221184]{2,1,0:T(2,128)(2,1)S(1)}, s32[16,3]{0,1:T(4,128)S(1)}, bf16[16,1,2,24576]{3,2,1,0:T(2,128)(2,1)}, s32[]{:T(128)}) while((s32[]{:T(128)}, bf16[1,2,221184]{2,1,0:T(2,128)(2,1)S(1)}, s32[16,3]{0,1:T(4,128)S(1)}, bf16[16,1,2,24576]{3,2,1,0:T(2,128)(2,1)}, s32[]{:T(128)}) %tuple.34), condition=%wide.while_cond, body=%wide.while_body.sunk | while | flops 2 | bytes 197729 | solution.py:58
  58.4 1.4 bitcast_dynamic-update-slice_fusion.2
  60.5 1.4 bitcast_dynamic-update-slice_fusion.2
  62.6 1.4 bitcast_dynamic-update-slice_fusion.2
  64.7 1.5 bitcast_dynamic-update-slice_fusion.2
  66.8 1.4 bitcast_dynamic-update-slice_fusion.2
  68.9 1.4 bitcast_dynamic-update-slice_fusion.2
  71.0 1.4 bitcast_dynamic-update-slice_fusion.2
  73.1 1.4 bitcast_dynamic-update-slice_fusion.2
  75.2 1.4 bitcast_dynamic-update-slice_fusion.2
  77.3 1.4 bitcast_dynamic-update-slice_fusion.2
  79.4 1.4 bitcast_dynamic-update-slice_fusion.2
  81.5 1.4 bitcast_dynamic-update-slice_fusion.2
  83.6 1.4 bitcast_dynamic-update-slice_fusion.2
  85.8 1.4 bitcast_dynamic-update-slice_fusion.2
  87.8 1.4 bitcast_dynamic-update-slice_fusion.2
  90.0 1.4 bitcast_dynamic-update-slice_fusion.2
  91.4 9.0 %all-to-all-start = ((bf16[1,16,2,24576]{3,2,0,1:T(2,128)(2,1)}), bf16[1,16,2,24576]{3,2,0,1:T(2,128)(2,1)S(1)}, u32[]{:S(2)}, u32[]{:S(2)}) async-start(bf16[1,16,2,24576]{3,2,0,1:T(2,128)(2,1)} %bitcast.4), calls=%async_computation | async-start | bytes 3145728 | tf_op jit(solution)/shard_map/all_to_all | solution.py:61
  101.1 35.8 %all-to-all-done = bf16[1,16,2,24576]{3,2,0,1:T(2,128)(2,1)S(1)} async-done(((bf16[1,16,2,24576]{3,2,0,1:T(2,128)(2,1)}), bf16[1,16,2,24576]{3,2,0,1:T(2,128)(2,1)S(1)}, u32[]{:S(2)}, u32[]{:S(2)}) %all-to-all-start) | async-done | bytes 1572896 | tf_op jit(solution)/shard_map/all_to_all | solution.py:61
  137.5 3.9 %fusion.2 = f32[32,24576]{1,0:T(8,128)} fusion(bf16[32,24576]{1,0:T(8,128)(2,1)S(1)} %reshape.55, bf16[1,32,24576]{2,1,0:T(8,128)(2,1)} %param.11, pred[24576]{0:T(1024)(128)(4,1)S(1)} %iota_compare_fusion, s32[32]{0:T(128)S(1)} %copy-done.4, s32[32]{0:T(128)S(1)} %copy-done.3), kind=kOutput, calls=%fused_computation.8 | convolution fusion | flops 52770816 | bytes 6316288 | tf_op jit(solution)/shard_map/ks,msc->mkc/dot_general | solution.py:72
  141.4 188.7 %all-reduce.8.cloned.1.call-done = f32[32,24576]{1,0:T(8,128)} async-done(((f32[32,24576]{1,0:T(8,128)}), f32[32,24576]{1,0:T(8,128)}) %all-reduce.8.cloned.1.call-update) | async-done | bytes 3145744 | tf_op jit(solution)/shard_map/psum | solution.py:74
  330.1 1.9 constant_dynamic-slice_fusion.1
  (138 shorter events, 59.2 us)
Async XLA Ops:
  6.5 0.9 copy-start.5
  6.5 0.7 copy-start.4
  7.6 3.1 copy-start
  10.7 1.4 copy-start.1
  13.5 1.4 copy-start.1
  16.2 1.4 copy-start.1
  19.0 1.4 copy-start.1
  21.7 1.4 copy-start.1
  24.5 1.4 copy-start.1
  27.2 1.4 copy-start.1
  30.0 1.4 copy-start.1
  32.7 1.4 copy-start.1
  35.5 1.4 copy-start.1
  38.2 1.4 copy-start.1
  41.0 1.4 copy-start.1
  43.7 1.4 copy-start.1
  46.5 1.4 copy-start.1
  49.2 1.4 copy-start.1
  52.0 1.4 copy-start.1
  54.7 0.7 copy-start.2
  91.4 45.4 %all-to-all-start = ((bf16[1,16,2,24576]{3,2,0,1:T(2,128)(2,1)}), bf16[1,16,2,24576]{3,2,0,1:T(2,128)(2,1)S(1)}, u32[]{:S(2)}, u32[]{:S(2)}) async-start(bf16[1,16,2,24576]{3,2,0,1:T(2,128)(2,1)} %bitcast.4), calls=%async_computation | async-start | bytes 3145728 | tf_op jit(solution)/shard_map/all_to_all | solution.py:61
  100.4 229.7 %all-reduce.8.cloned.1.call-start = ((), (), s32[]{:S(2)}) async-start(), calls=%async_computation.1 | async-start | bytes 6291456 | tf_op jit(solution)/shard_map/psum | solution.py:74
  101.1 36.4 %copy-start.3 = (s32[32]{0:T(128)S(1)}, s32[32]{0:T(128)}, u32[]{:S(2)}) copy-start(s32[32]{0:T(128)} %param.17) | copy-start | bytes 388
Sparse Core Ops, SparseCore 0:
  141.5 188.5 all-reduce.7
where the time goes:
time: 340 us; the launch traced here: 339 us
  waiting for transfers between devices  225 us (66%)
  local copies, waits for them, and re-layouts  53.2 us (16%)
  other arithmetic  34.1 us (10%)
  between operations  13.5 us (4%)
  starting transfers between devices  9.03 us (3%)
  matrix products  3.87 us (1%)
    psum x1, waiting for transfers between devices, body(): lax.psum(jnp.where(valid_cols[None, :], jnp.sum(pert_rows * spread, axis=...  189 us
    all_to_all x1, waiting for transfers between devices, body(): lax.all_to_all(outgoing, 'lev', split_axis=1, concat_axis=1, tiled=True)  35.8 us
    gather x48, local copies, waits for them, and re-layouts  33.6 us
    add x16, other arithmetic, step_once(): return state + change  15.1 us
    while x32, local copies, waits for them, and re-layouts  14.3 us
    all_to_all x1, starting transfers between devices, body(): lax.all_to_all(outgoing, 'lev', split_axis=1, concat_axis=1, tiled=True)  8.99 us
    mul x16, other arithmetic, step_once(): flux_y = scaled_y[:, :-1] * (state[:, 1:] - state[:, :-1])  8.01 us
  transfers between devices with their start and end apart: 2, of which 2 were waited for; matrix products, arithmetic and copies ran while one was open for 0% of the time, Pallas kernels for 0%

commit v1 on v0

--- a/solution.py
+++ b/solution.py
@@ -71,8 +71,11 @@
     share_rows = levels // member_devices
     spread = jnp.einsum("ks,msc->mkc", permuted, arrived, preferred_element_type=jnp.float32)
     pert_rows = perturbations.astype(jnp.float32)
-    summed = lax.psum(
-        jnp.where(valid_cols[None, :], jnp.sum(pert_rows * spread, axis=0), 0.0), "mem"
+    summed = jnp.sum(
+        lax.all_gather(
+            jnp.where(valid_cols[None, :], jnp.sum(pert_rows * spread, axis=0), 0.0), "mem"
+        ),
+        axis=0,
     )
     result = lax.dynamic_slice_in_dim(summed, lax.axis_index("mem") * share_rows, share_rows, 0)
     return result

time: 340 us -> 610 us (1.79)
  waiting for transfers between devices: 225 us -> 479 us
  other arithmetic: 34.1 us -> 51.1 us
    all_gather x0 -> x1, waiting for transfers between devices: none -> 443 us  [body(): lax.all_gather(jnp.where(valid_cols[None, :], jnp.sum(pert_rows * spread,...]
    psum x1 -> x0, waiting for transfers between devices: 189 us -> none  [body(): lax.psum(jnp.where(valid_cols[None, :], jnp.sum(pert_rows * spread, axis=...]
    reduce_sum x0 -> x1, other arithmetic: none -> 17 us  [body(): jnp.sum(lax.all_gather(jnp.where(valid_cols[None, :], jnp.sum(pert_rows *...]
where the time goes in v1:
time: 610 us; the launch traced here: 608 us
  waiting for transfers between devices  479 us (79%)
  other arithmetic  51.1 us (8%)
  local copies, waits for them, and re-layouts  50.9 us (8%)
  between operations  13.5 us (2%)
  starting transfers between devices  9.03 us (1%)
    all_gather x1, waiting for transfers between devices, body(): lax.all_gather(jnp.where(valid_cols[None, :], jnp.sum(pert_rows * spread,...  443 us
    all_to_all x1, waiting for transfers between devices, body(): lax.all_to_all(outgoing, 'lev', split_axis=1, concat_axis=1, tiled=True)  35.8 us
    gather x48, local copies, waits for them, and re-layouts  32.5 us
    reduce_sum x1, other arithmetic, body(): jnp.sum(lax.all_gather(jnp.where(valid_cols[None, :], jnp.sum(pert_rows *...  17 us
    add x16, other arithmetic, step_once(): return state + change  15.1 us
    while x32, local copies, waits for them, and re-layouts  14.3 us
  transfers between devices with their start and end apart: 2, of which 2 were waited for; matrix products, arithmetic and copies ran while one was open for 0% of the time, Pallas kernels for 0%

profile of v1, /device:TPU:8, one launch (start us, length us, event | category | flops | bytes accessed | tf_op | source)
XLA Modules:
  0.0 607.8 jit_solution(9345515661546686561)
XLA Ops:
  8.5 3.1 broadcast_multiply_fusion
  11.6 44.0 %while.11 = (s32[]{:T(128)}, f32[1,2,384,512]{3,2,1,0:T(8,128)S(1)}, f32[2,384,512]{2,1,0:T(8,128)}, f32[2,384,512]{2,1,0:T(8,128)S(1)}, s32[]{:T(128)}) while((s32[]{:T(128)}, f32[1,2,384,512]{3,2,1,0:T(8,128)S(1)}, f32[2,384,512]{2,1,0:T(8,128)}, f32[2,384,512]{2,1,0:T(8,128)S(1)}, s32[]{:T(128)}) %tuple.39), condition=%wide.region_4.5_spmd, body=%wide.region_3.4_spmd.sunk | while | flops 3142146 | bytes 25130072 | solution.py:22
  56.3 1.4 pad.9
  57.7 32.5 %while.12 = (s32[]{:T(128)}, bf16[1,2,221184]{2,1,0:T(2,128)(2,1)S(1)}, s32[16,3]{0,1:T(4,128)S(1)}, bf16[16,1,2,24576]{3,2,1,0:T(2,128)(2,1)}, s32[]{:T(128)}) while((s32[]{:T(128)}, bf16[1,2,221184]{2,1,0:T(2,128)(2,1)S(1)}, s32[16,3]{0,1:T(4,128)S(1)}, bf16[16,1,2,24576]{3,2,1,0:T(2,128)(2,1)}, s32[]{:T(128)}) %tuple.34), condition=%wide.while_cond, body=%wide.while_body.sunk | while | flops 2 | bytes 197229 | solution.py:58
  60.4 1.4 bitcast_dynamic-update-slice_fusion.2
  62.4 1.4 bitcast_dynamic-update-slice_fusion.2
  64.5 1.4 bitcast_dynamic-update-slice_fusion.2
  66.5 1.4 bitcast_dynamic-update-slice_fusion.2
  68.5 1.4 bitcast_dynamic-update-slice_fusion.2
  70.6 1.4 bitcast_dynamic-update-slice_fusion.2
  72.6 1.4 bitcast_dynamic-update-slice_fusion.2
  74.6 1.4 bitcast_dynamic-update-slice_fusion.2
  76.7 1.4 bitcast_dynamic-update-slice_fusion.2
  78.7 1.4 bitcast_dynamic-update-slice_fusion.2
  80.7 1.4 bitcast_dynamic-update-slice_fusion.2
  82.7 1.4 bitcast_dynamic-update-slice_fusion.2
  84.8 1.4 bitcast_dynamic-update-slice_fusion.2
  86.8 1.4 bitcast_dynamic-update-slice_fusion.2
  88.8 1.4 bitcast_dynamic-update-slice_fusion.2
  90.3 9.0 %all-to-all-start = ((bf16[1,16,2,24576]{3,2,0,1:T(2,128)(2,1)}), bf16[1,16,2,24576]{3,2,0,1:T(2,128)(2,1)S(1)}, u32[]{:S(2)}, u32[]{:S(2)}) async-start(bf16[1,16,2,24576]{3,2,0,1:T(2,128)(2,1)} %bitcast.4), calls=%async_computation | async-start | bytes 3145728 | tf_op jit(solution)/shard_map/all_to_all | solution.py:61
  99.9 35.8 %all-to-all-done = bf16[1,16,2,24576]{3,2,0,1:T(2,128)(2,1)S(1)} async-done(((bf16[1,16,2,24576]{3,2,0,1:T(2,128)(2,1)}), bf16[1,16,2,24576]{3,2,0,1:T(2,128)(2,1)S(1)}, u32[]{:S(2)}, u32[]{:S(2)}) %all-to-all-start) | async-done | bytes 1572896 | tf_op jit(solution)/shard_map/all_to_all | solution.py:61
  136.3 3.8 fusion.1
  140.1 443.0 %all-gather.2.cloned.1.call-done = f32[16,32,24576]{2,1,0:T(8,128)} async-done(((f32[1,32,24576]{2,1,0:T(8,128)}), f32[16,32,24576]{2,1,0:T(8,128)}) %all-gather.2.cloned.1.call-update) | async-done | bytes 50331664 | tf_op jit(solution)/shard_map/all_gather | solution.py:75
  583.1 17.0 %reduce_sum.43 = f32[32,24576]{1,0:T(8,128)S(1)} reduce(f32[16,32,24576]{2,1,0:T(8,128)} %all-gather.2.cloned.1.call-done, f32[]{:T(128)} %constant.17.clone.1), dimensions={0}, to_apply=%region_6.7 | reduce | flops 11796480 | bytes 53477380 | tf_op jit(solution)/shard_map/reduce_sum | solution.py:74
  (139 shorter events, 59.2 us)
Async XLA Ops:
  6.5 1.7 copy-start.5
  6.5 1.5 copy-start.4
  6.5 0.7 copy-start.2
  8.4 3.1 copy-start
  11.6 1.4 copy-start.1
  14.3 1.4 copy-start.1
  17.1 1.4 copy-start.1
  19.8 1.4 copy-start.1
  22.6 1.4 copy-start.1
  25.3 1.4 copy-start.1
  28.1 1.4 copy-start.1
  30.9 1.4 copy-start.1
  33.6 1.4 copy-start.1
  36.4 1.4 copy-start.1
  39.1 1.4 copy-start.1
  41.9 1.4 copy-start.1
  44.6 1.4 copy-start.1
  47.4 1.4 copy-start.1
  50.1 1.4 copy-start.1
  52.9 1.4 copy-start.1
  90.3 45.4 %all-to-all-start = ((bf16[1,16,2,24576]{3,2,0,1:T(2,128)(2,1)}), bf16[1,16,2,24576]{3,2,0,1:T(2,128)(2,1)S(1)}, u32[]{:S(2)}, u32[]{:S(2)}) async-start(bf16[1,16,2,24576]{3,2,0,1:T(2,128)(2,1)} %bitcast.4), calls=%async_computation | async-start | bytes 3145728 | tf_op jit(solution)/shard_map/all_to_all | solution.py:61
  99.3 483.9 %all-gather.2.cloned.1.call-start = ((), (), s32[]{:S(2)}) async-start(), calls=%async_computation.1 | async-start | bytes 53477376 | tf_op jit(solution)/shard_map/all_gather | solution.py:75
  99.9 36.5 %copy-start.3 = (s32[32]{0:T(128)S(1)}, s32[32]{0:T(128)}, u32[]{:S(2)}) copy-start(s32[32]{0:T(128)} %param.17) | copy-start | bytes 388
Sparse Core Ops, SparseCore 0:
  140.3 442.8 all-gather.1
